TPU v7x, 32 devices: a whole 2x2x4 slice. The times are simulated.
32 devices in a mesh: groups: 2 (over y), tiles: 4 (over z), freq: 2 (over x), field: 2 (over core).
Axes of the slice: x: 2, y: 2, z: 4, core: 2. Of those that a mesh axis runs over, the one named last changes fastest.
Arguments:
- fields: bfloat16 [2, 4, 512, 1024], P('field', 'tiles', ('groups', 'freq')), parts along dimension 2, may hold values from -7.5 to 7.5
- slot_tile_ids: int32 [4], replicated, may hold values from 0 to 3, each once
- neighbour_tile_ids: int32 [4, 4], replicated, may hold values from 0 to 3
- neighbour_rotation_code: int32 [4, 4], replicated, may hold values from 0 to 7
- paired_tile_ids: int32 [4, 2], P('tiles'), may hold values from 0 to 3
Outputs:
- csd: float32 [8, 2, 2, 32, 128, 128], P(('groups', 'tiles'), None, None, ('freq', 'field')), parts along dimension 0
There are 2 independent parts, one for each index of `groups`. A program takes and returns all parts, laid end to end along the dimension named above; an argument that names none is the same for every part. Nothing has to cross between parts.
All inputs are finite; a program needn't handle non-finite values.
Results may differ from a plain program's by a relative error of at most 0.0095.
Values may be sent and summed in bfloat16 or wider, within the bound.
A program may use at most 64 MiB of HBM per device.

v0:
```python
import math

import jax
import jax.numpy as jnp
from jax import lax
from jax.sharding import PartitionSpec as P

SIDE = 32
SEGLEN = 64


diffusion = 0.25


def slot_lookup(slot_tile_ids, tile_ids):
    matches = (slot_tile_ids[None, :] == tile_ids.reshape(-1)[:, None]).astype(jnp.int32)
    positions = jnp.sum(
        matches * jnp.arange(slot_tile_ids.shape[0], dtype=jnp.int32)[None, :], axis=1
    )
    return positions.reshape(tile_ids.shape)


def tile_edges(field, tile_side):
    cell_count = field.shape[-1]
    north = field[..., :tile_side]
    east = field[..., tile_side - 1 :: tile_side]
    south = field[..., cell_count - tile_side :]
    west = field[..., ::tile_side]
    return jnp.stack([north, east, south, west], axis=-3)


def inner_edges(field, tile_side):
    cell_count = field.shape[-1]
    north = field[..., tile_side : 2 * tile_side]
    east = field[..., tile_side - 2 :: tile_side]
    south = field[..., cell_count - 2 * tile_side : cell_count - tile_side]
    west = field[..., 1::tile_side]
    return jnp.stack([north, east, south, west], axis=-3)


def pick_rims(all_edges, near_slots, codes):
    chosen = all_edges[near_slots, codes % 4]
    flipped = chosen[..., ::-1]
    return jnp.where((codes // 4 == 1)[:, :, None, None], flipped, chosen)


def smooth_step(field, rims, tile_side):
    cell_count = field.shape[-1]
    values = field.astype(jnp.float32)
    edge_vals = rims.astype(jnp.float32)
    above_row = jnp.concatenate([edge_vals[:, 0], values[..., : cell_count - tile_side]], axis=-1)
    below_row = jnp.concatenate([values[..., tile_side:], edge_vals[:, 2]], axis=-1)
    column_pos = jnp.arange(cell_count, dtype=jnp.int32) % tile_side
    west_full = jnp.repeat(edge_vals[:, 3], tile_side, axis=-1)
    east_full = jnp.repeat(edge_vals[:, 1], tile_side, axis=-1)
    leftward = jnp.where(column_pos == 0, west_full, jnp.roll(values, 1, axis=-1))
    rightward = jnp.where(column_pos == tile_side - 1, east_full, jnp.roll(values, -1, axis=-1))
    laplace = above_row + below_row + leftward + rightward - 4.0 * values
    return (values + diffusion * laplace).astype(jnp.bfloat16)


def before_along(values, first):
    return jnp.concatenate([first[..., None], values[..., :-1]], axis=-1)


def after_along(values, last):
    return jnp.concatenate([values[..., 1:], last[..., None]], axis=-1)


def smooth_one(values, above, below, leftward, rightward):
    laplace = above + below + leftward + rightward - 4.0 * values
    return (values + diffusion * laplace).astype(jnp.bfloat16)


def edge_sweep(outer, inner, rims):
    outer_vals = outer.astype(jnp.float32)
    inner_vals = inner.astype(jnp.float32)
    rim_vals = rims.astype(jnp.float32)
    north_rim = rim_vals[:, 0]
    east_rim = rim_vals[:, 1]
    south_rim = rim_vals[:, 2]
    west_rim = rim_vals[:, 3]
    north = outer_vals[:, 0]
    east = outer_vals[:, 1]
    south = outer_vals[:, 2]
    west = outer_vals[:, 3]
    new_north = smooth_one(
        north,
        north_rim,
        inner_vals[:, 0],
        before_along(north, west_rim[..., 0]),
        after_along(north, east_rim[..., 0]),
    )
    new_east = smooth_one(
        east,
        before_along(east, north_rim[..., -1]),
        after_along(east, south_rim[..., -1]),
        inner_vals[:, 1],
        east_rim,
    )
    new_south = smooth_one(
        south,
        inner_vals[:, 2],
        south_rim,
        before_along(south, west_rim[..., -1]),
        after_along(south, east_rim[..., -1]),
    )
    new_west = smooth_one(
        west,
        before_along(west, north_rim[..., 0]),
        after_along(west, south_rim[..., 0]),
        west_rim,
        inner_vals[:, 3],
    )
    return jnp.stack([new_north, new_east, new_south, new_west], axis=1)


def coarse_sums(field, tile_side):
    leading = field.shape[:-1]
    blocks = field.astype(jnp.float32).reshape(leading + (tile_side // 2, 2, tile_side // 4, 4))
    return jnp.sum(blocks, axis=(-3, -1)).reshape(leading + (tile_side // 2 * (tile_side // 4),))


def window_table(seg_length):
    samples = jnp.arange(seg_length, dtype=jnp.int32)
    frequency = jnp.arange(seg_length // 2, dtype=jnp.int32)
    products = frequency[:, None] * samples[None, :] % seg_length
    angles = 2.0 * math.pi / seg_length * products.astype(jnp.float32)
    window = 0.5 - 0.5 * jnp.cos(2.0 * math.pi / seg_length * samples.astype(jnp.float32))
    dft_table = jnp.stack([window[None, :] * jnp.cos(angles), -window[None, :] * jnp.sin(angles)])
    return (dft_table, jnp.sum(window * window))


def segment_spectra(coarse, dft_table):
    leading = coarse.shape[0]
    segments = coarse.reshape(leading, -1, dft_table.shape[-1], coarse.shape[-1])
    spectra = jnp.einsum("cft,nstp->nscfp", dft_table, segments, precision=lax.Precision.HIGHEST)
    return spectra.astype(jnp.bfloat16)


def cross_density(height, partner, window_power):
    rotated = jnp.stack([height[:, :, 1], -height[:, :, 0]], axis=2)
    stacked = jnp.stack([height, rotated], axis=1)
    cross = jnp.einsum(
        "noscfi,nkscfj->nkofij", stacked, partner, preferred_element_type=jnp.float32
    )
    return cross / (partner.shape[2] * window_power)


def shards(fields, slot_tile_ids, neighbour_tile_ids, neighbour_rotation_code, paired_tile_ids):
    field = fields[0]
    local_count = field.shape[0]
    first_local = lax.axis_index("tiles") * local_count
    near_all = slot_lookup(slot_tile_ids, neighbour_tile_ids)
    near_local = lax.dynamic_slice_in_dim(near_all, first_local, local_count, 0)
    code_local = lax.dynamic_slice_in_dim(neighbour_rotation_code, first_local, local_count, 0)
    every_outer = lax.all_gather(tile_edges(field, SIDE), "tiles", axis=0, tiled=True)
    every_inner = lax.all_gather(inner_edges(field, SIDE), "tiles", axis=0, tiled=True)
    every_rim = pick_rims(every_outer, near_all, neighbour_rotation_code)
    local_rim = lax.dynamic_slice_in_dim(every_rim, first_local, local_count, 0)
    field = smooth_step(field, local_rim, SIDE)
    new_edges = edge_sweep(every_outer, every_inner, every_rim)
    field = smooth_step(field, pick_rims(new_edges, near_local, code_local), SIDE)
    dft_table, window_power = window_table(SEGLEN)
    spectra = segment_spectra(coarse_sums(field, SIDE), dft_table)
    banded = lax.all_to_all(
        lax.all_to_all(spectra[None], "freq", split_axis=4, concat_axis=2, tiled=True),
        "field",
        split_axis=4,
        concat_axis=0,
        tiled=True,
    )
    partner_slots = slot_lookup(slot_tile_ids, paired_tile_ids)
    every_band = lax.all_gather(banded, "tiles", axis=1, tiled=True)
    first_slot = lax.axis_index("tiles") * banded.shape[1]
    height = lax.dynamic_slice_in_dim(every_band[0], first_slot, banded.shape[1], 0)
    velocity = every_band[1]
    return cross_density(height, velocity[partner_slots], window_power)


def solution(mesh):
    placed = (P("field", "tiles", ("groups", "freq"), None), P(), P(), P(), P("tiles", None))
    return jax.shard_map(
        shards,
        mesh=mesh,
        in_specs=placed,
        out_specs=P(("groups", "tiles"), None, None, ("freq", "field"), None, None),
        check_vma=False,
    )
```

profile of v0, /device:TPU:0, one launch (start us, length us, event | category | flops | bytes accessed | tf_op | source)
XLA Modules:
  0.0 69.6 jit_solution(6394495090829797569)
XLA Ops:
  0.1 0.8 %eq.65 = s32[16]{0:T(128)S(1)} reshape(s32[4,4]{1,0:T(4,128)} %param.7) | data formatting | bytes 128 | tf_op jit(solution)/shard_map/eq | solution.py:16
  0.9 0.7 %select_reduce_fusion = s32[16]{0:T(128)S(1)} fusion(s32[16]{0:T(128)S(1)} %eq.65, s32[4]{0:T(128)} %param.6), kind=kLoop, calls=%fused_computation.163 | loop fusion | flops 176 | bytes 144 | tf_op jit(solution)/shard_map/reduce_sum | solution.py:17
  1.9 1.1 %copy.181 = bf16[1,1,128,1024]{2,3,1,0:T(8,128)(2,1)S(1)} copy(bf16[1,1,128,1024]{3,2,1,0:T(8,128)(2,1)} %param.5) | data formatting | bytes 524288 | tf_op args[0]
  3.3 1.0 %fusion.83 = (f32[1,128,992]{1,2,0:T(8,128)}, f32[1,128,992]{1,2,0:T(8,128)}) fusion(f32[1,128,1024]{1,2,0:T(8,128)S(1)} %bitcast_convert_fusion), kind=kLoop, calls=%fused_computation.197 | loop fusion | bytes 2031616 | tf_op jit(solution)/shard_map/slice | solution.py:51
  4.6 15.1 %all_gather.9 = bf16[4,4,128,32]{2,3,1,0:T(8,128)(2,1)S(1)} all-gather(bf16[1,4,128,32]{2,3,1,0:T(8,128)(2,1)S(1)} %pad_maximum_fusion.5), channel_id=1, replica_groups=mesh['groups'=2,'tiles'=4,'freq'=2,'field'=2] {'tiles'}, dimensions={0}, use_global_device_ids=true | all-gather | bytes 163840 | tf_op jit(solution)/shard_map/all_gather | solution.py:157
  19.7 0.6 gather_fusion
  20.5 2.2 %fusion.14 = (f32[1,128,1024]{1,2,0:T(8,128)S(1)}, f32[1,128,1024]{1,2,0:T(8,128)S(1)}, f32[1,128,1024]{1,2,0:T(8,128)S(1)}, f32[1,128,1024]{1,2,0:T(8,128)S(1)}) fusion(f32[128,32]{0,1:T(8,128)S(1)} %get-tuple-element.45, f32[128,32]{0,1:T(8,128)S(1)} %get-tuple-element.44, pred[1024]{0:T(1024)(128)(4,1)S(1)} %get-tuple-element.75, ...), kind=kLoop, calls=%fused_computation.32 | loop fusion | flops 2097152 | bytes 4491264 | tf_op jit(solution)/shard_map/convert_element_type | solution.py:49
  22.7 1.0 %fusion.80 = (f32[1,128,992]{1,2,0:T(8,128)}, f32[1,128,992]{1,2,0:T(8,128)}) fusion(f32[1,128,1024]{1,2,0:T(8,128)S(1)} %get-tuple-element.9), kind=kLoop, calls=%fused_computation.194 | loop fusion | bytes 2031616 | tf_op jit(solution)/shard_map/slice | solution.py:52
  23.8 13.5 %all_gather.10 = bf16[4,4,128,32]{2,3,1,0:T(8,128)(2,1)S(1)} all-gather(bf16[1,4,128,32]{2,3,1,0:T(8,128)(2,1)S(1)} %pad_maximum_fusion.6), channel_id=1, replica_groups=mesh['groups'=2,'tiles'=4,'freq'=2,'field'=2] {'tiles'}, dimensions={0}, use_global_device_ids=true | all-gather | bytes 163840 | tf_op jit(solution)/shard_map/all_gather | solution.py:158
  37.7 0.6 gather_fusion.1
  38.5 1.2 %maximum_add_fusion.1 = f32[1,128,1024]{1,2,0:T(8,128)S(1)} fusion(f32[1,128,992]{1,2,0:T(8,128)} %get-tuple-element.22, f32[1,128,32]{1,2,0:T(8,128)S(1)} %get-tuple-element.52, f32[1,128,32]{1,2,0:T(8,128)S(1)} %get-tuple-element.51, f32[1,128,992]{1,2,0:T(8,128)} %get-tuple-element.21), kind=kLoop, calls=%fused_computation.20 | loop fusion | flops 393216 | bytes 1572864 | tf_op jit(solution)/shard_map/add | solution.py:58
  39.8 1.3 %convert_reduce_fusion = f32[128,16,8]{0,2,1:T(8,128)S(1)} fusion(f32[1,128,16,2,8,4]{1,5,4,3,2,0:T(4,128)S(1)} %bitcast.265, f32[128,16,2]{0,2,1:T(2,128)S(1)} %bitcast.274, f32[1,128,16,2,8,4]{1,5,4,3,2,0:T(4,128)S(1)} %bitcast.263, f32[1,128,16,2,8,4]{1,5,4,3,2,0:T(4,128)S(1)} %bitcast.264, f32[128,16,2]{0,2,1:T(2,128)S(1)} %bitcast.273, ...), kind=kLoop, calls=%fused_computation.31 | loop fusion | flops 2867200 | bytes 3540992 | tf_op jit(solution)/shard_map/reduce_sum | solution.py:121
  41.1 0.1 reshape.897
  41.3 0.3 fusion.1
  41.6 0.6 copy.200
  42.2 3.3 %all-to-all-start = ((bf16[1,1,2,2,32,128]{5,3,2,1,0,4:T(2,128)(2,1)}), bf16[1,1,2,2,32,128]{5,3,2,1,0,4:T(2,128)(2,1)S(1)}, u32[]{:S(2)}, u32[]{:S(2)}) async-start(bf16[1,1,2,2,32,128]{5,3,2,1,0,4:T(2,128)(2,1)} %copy.200), calls=%async_computation | async-start | bytes 65536 | tf_op jit(solution)/shard_map/all_to_all | solution.py:167
  45.5 0.2 fusion.70
  45.7 0.7 multiply_reduce_fusion
  47.0 2.4 %all-to-all-done = bf16[1,1,2,2,32,128]{5,3,2,1,0,4:T(2,128)(2,1)S(1)} async-done(((bf16[1,1,2,2,32,128]{5,3,2,1,0,4:T(2,128)(2,1)}), bf16[1,1,2,2,32,128]{5,3,2,1,0,4:T(2,128)(2,1)S(1)}, u32[]{:S(2)}, u32[]{:S(2)}) %all-to-all-start) | async-done | bytes 32800 | tf_op jit(solution)/shard_map/all_to_all | solution.py:167
  49.5 3.7 %all_to_all.36 = bf16[1,1,4,2,16,128]{5,3,2,1,0,4:T(2,128)(2,1)S(1)} all-to-all(bf16[1,1,4,2,16,128]{5,3,2,1,0,4:T(2,128)(2,1)S(1)} %copy.203), channel_id=1, replica_groups=mesh['groups'=2,'tiles'=4,'freq'=2,'field'=2] {'field'}, dimensions={4} | all-to-all | bytes 65536 | tf_op jit(solution)/shard_map/all_to_all | solution.py:166
  53.2 13.4 %all-gather = bf16[2,4,1,4,2,8,128]{6,5,4,3,1,2,0:T(8,128)(2,1)S(1)} all-gather(bf16[2,1,1,4,2,8,128]{6,5,4,3,1,2,0:T(8,128)(2,1)S(1)} %bitcast.267), channel_id=2, replica_groups=mesh['groups'=2,'tiles'=4,'freq'=2,'field'=2] {'tiles'}, dimensions={1}, use_global_device_ids=true | all-gather | bytes 163840 | tf_op jit(solution)/shard_map/all_gather | solution.py:174
  66.7 0.6 gather_fusion.2
  67.3 0.5 fusion
  67.8 1.8 %copy.209 = f32[1,2,2,8,128,128]{5,4,3,2,1,0:T(8,128)} copy(f32[1,2,2,8,128,128]{4,5,2,1,3,0:T(8,128)S(1)} %fusion) | data formatting | bytes 4194304 | tf_op jit(solution)/shard_map/div | solution.py:147
  (65 shorter events, 1.9 us)
Async XLA Ops:
  3.3 1.1 %copy-start = (s32[4,4]{1,0:T(4,128)S(1)}, s32[4,4]{1,0:T(4,128)}, u32[]{:S(2)}) copy-start(s32[4,4]{1,0:T(4,128)} %param.8) | copy-start | bytes 196
  39.8 5.7 %copy-start.1 = (s32[4]{0:T(128)S(1)}, s32[4]{0:T(128)}, u32[]{:S(2)}) copy-start(s32[4]{0:T(128)} %param.6) | copy-start | bytes 52
  39.8 5.7 %copy-start.2 = (s32[1,2]{1,0:T(1,128)S(1)}, s32[1,2]{1,0:T(1,128)}, u32[]{:S(2)}) copy-start(s32[1,2]{1,0:T(1,128)} %param.9) | copy-start | bytes 28
  42.2 7.2 %all-to-all-start = ((bf16[1,1,2,2,32,128]{5,3,2,1,0,4:T(2,128)(2,1)}), bf16[1,1,2,2,32,128]{5,3,2,1,0,4:T(2,128)(2,1)S(1)}, u32[]{:S(2)}, u32[]{:S(2)}) async-start(bf16[1,1,2,2,32,128]{5,3,2,1,0,4:T(2,128)(2,1)} %copy.200), calls=%async_computation | async-start | bytes 65536 | tf_op jit(solution)/shard_map/all_to_all | solution.py:167
where the time goes:
time: 70 us; the launch traced here: 69.6 us
  blocking collectives  45.8 us (65%)
  local copies, waits for them, and re-layouts  9.18 us (13%)
  other arithmetic  7.23 us (10%)
  starting transfers between devices  3.26 us (5%)
  waiting for transfers between devices  2.42 us (3%)
  between operations  1.03 us (1%)
  matrix products  0.77 us (1%)
    all_gather x1, blocking collectives, shards(): lax.all_gather(tile_edges(field, SIDE), 'tiles', axis=0, tiled=True)  15.1 us
    all_gather x1, blocking collectives, shards(): lax.all_gather(inner_edges(field, SIDE), 'tiles', axis=0, tiled=True)  13.5 us
    all_gather x1, blocking collectives, shards(): every_band = lax.all_gather(banded, 'tiles', axis=1, tiled=True)  13.4 us
    all_to_all x1, blocking collectives, shards(): lax.all_to_all(lax.all_to_all(spectra[None], 'freq', split_axis=4, concat...  3.75 us
    all_to_all x1, starting transfers between devices, shards(): lax.all_to_all(spectra[None], 'freq', split_axis=4, concat_axis=2, tiled=...  3.26 us
    all_to_all x1, waiting for transfers between devices, shards(): lax.all_to_all(spectra[None], 'freq', split_axis=4, concat_axis=2, tiled=...  2.42 us
    convert_element_type x2, other arithmetic, smooth_step(): values = field.astype(jnp.float32)  2.21 us
    div x1, local copies, waits for them, and re-layouts, cross_density(): return cross / (partner.shape[2] * window_power)  1.81 us
  transfers between devices with their start and end apart: 1, of which 1 were waited for; matrix products, arithmetic and copies ran while one was open for 1% of the time, Pallas kernels for 0%

commit v1 on v0

v1 whole, which is shorter than its diff:
```python
import functools

import jax
import jax.numpy as jnp
import numpy as np
from jax import lax
from jax.experimental import pallas as pl
from jax.experimental.pallas import tpu as pltpu
from jax.sharding import PartitionSpec as P

SIDE = 32
SEGLEN = 64
CELLS = SIDE * SIDE
EDGE = 4 * SIDE
PAIRS = EDGE // 2
COARSE = CELLS // 8
MESH = pl.DeviceIdType.MESH


def smooth_cells(field, rims):
    padded = np.zeros(field.shape[:-2] + (SIDE + 2, SIDE + 2))
    padded[..., 1:-1, 1:-1] = field
    padded[..., 0, 1:-1] = rims[..., 0, :]
    padded[..., 1:-1, -1] = rims[..., 1, :]
    padded[..., -1, 1:-1] = rims[..., 2, :]
    padded[..., 1:-1, 0] = rims[..., 3, :]
    around = padded[..., :-2, 1:-1] + padded[..., 2:, 1:-1] + padded[..., 1:-1, :-2] + padded[..., 1:-1, 2:]
    return 0.25 * around


def coarse_cells(field):
    blocks = field.reshape(field.shape[:-2] + (SIDE // 2, 2, SIDE // 4, 4))
    return blocks.sum(axis=(-3, -1)).reshape(field.shape[:-2] + (COARSE,))


def edges_of(field):
    return np.stack([field[..., 0, :], field[..., :, -1], field[..., -1, :], field[..., :, 0]], axis=-2)


def edge_pairs(field):
    edges = edges_of(field)
    return edges.reshape(edges.shape[:-2] + (PAIRS, 2)).sum(axis=-1)


def spatial_tables():
    cells = np.eye(CELLS).reshape(CELLS, SIDE, SIDE)
    rims = np.eye(EDGE).reshape(EDGE, 4, SIDE)
    cell_zero = np.zeros((EDGE, SIDE, SIDE))
    rim_zero = np.zeros((CELLS, 4, SIDE))
    once = smooth_cells(cells, rim_zero)
    rim_once = smooth_cells(cell_zero, rims)
    own_coarse = coarse_cells(smooth_cells(once, rim_zero))
    outer = edges_of(cells).reshape(CELLS, EDGE)
    own_pairs = edge_pairs(once)
    sender = np.concatenate([own_coarse, outer, own_pairs, own_pairs], axis=1)
    rim_coarse = coarse_cells(smooth_cells(rim_once, np.zeros((EDGE, 4, SIDE)))).T
    rim_pairs = edge_pairs(rim_once).T
    pair_rims = np.repeat(np.eye(PAIRS), 2, axis=1).reshape(PAIRS, 4, SIDE)
    pair_coarse = coarse_cells(smooth_cells(np.zeros((PAIRS, SIDE, SIDE)), pair_rims)).T * 0.5
    pair_coarse = pair_coarse * 1.0
    flip = np.kron(np.eye(4), np.eye(SIDE)[::-1])
    pair_flip = np.kron(np.eye(4), np.eye(SIDE // 2)[::-1])
    both = np.concatenate([np.eye(EDGE), flip])
    pair_both = np.concatenate([np.eye(PAIRS), pair_flip])
    pair_own = np.concatenate([pair_both, pair_both], axis=1)
    pair_rim = pair_both @ rim_pairs
    pair_coarse = np.concatenate([pair_coarse, np.zeros((COARSE, EDGE - PAIRS))], axis=1)
    receiver = np.concatenate([both, pair_own, pair_rim, rim_coarse, pair_coarse, np.eye(COARSE)])
    return sender.astype(jnp.bfloat16), receiver.astype(jnp.bfloat16)


def hann():
    return 0.5 - 0.5 * np.cos(2.0 * np.pi * np.arange(SEGLEN) / SEGLEN)


def time_table(segments, bands):
    per_band = SEGLEN // 2 // bands
    window = hann()
    table = np.zeros((bands, 2, segments, per_band, segments, SEGLEN))
    for band in range(bands):
        for inner in range(per_band):
            angles = 2.0 * np.pi * (((band * per_band + inner) * np.arange(SEGLEN)) % SEGLEN) / SEGLEN
            for segment in range(segments):
                table[band, 0, segment, inner, segment] = window * np.cos(angles)
                table[band, 1, segment, inner, segment] = -window * np.sin(angles)
    return table.reshape(bands * 2 * segments * per_band, segments * SEGLEN).astype(np.float32)


def repeat(count, body):
    if count <= 4:
        for step in range(count):
            body(step)
    else:
        lax.fori_loop(0, count, lambda step, carry: (body(step), carry)[1], 0)


def exchange_kernel(nz, nf, rows, packed, field_ref, spatial_ref, time_ref, out_ref, send, send_sem, recv_sem, own_sem):
    group = lax.axis_index("groups")
    my_z = lax.axis_index("tiles")
    my_f = lax.axis_index("freq")
    my_c = lax.axis_index("field")
    last = send.shape[1]
    bands = 2 * nf

    def peers(dz, visit):
        z = lax.rem(my_z + dz, nz)
        for df in range(nf):
            for dc in range(2):
                yield_at = df * 2 + dc
                f = lax.rem(my_f + df, nf)
                c = lax.rem(my_c + dc, 2)
                visit(dz, yield_at, z, f, c)

    def each_peer(visit):
        def same(dz, where, z, f, c):
            if where:
                visit(True, dz, where, z, f, c)

        peers(0, same)
        repeat(nz - 1, lambda step: peers(step + 1, functools.partial(visit, False)))

    barrier = pltpu.get_barrier_semaphore()

    def greet(near, dz, where, z, f, c):
        pl.semaphore_signal(barrier, inc=1, device_id=(group, z, f, c), device_id_type=MESH)

    each_peer(greet)

    mapped = jnp.dot(field_ref[...], spatial_ref[...], preferred_element_type=jnp.float32)
    spectra = jnp.dot(
        time_ref[...], mapped, precision=lax.Precision.HIGHEST, preferred_element_type=jnp.float32
    )
    half = rows // 2
    lane = lax.broadcasted_iota(jnp.int32, (half, EDGE), 1)
    for band in range(bands):
        block = spectra[band * rows : (band + 1) * rows]
        send[band, 0:rows, :] = block[:, 0:COARSE].astype(jnp.bfloat16)
        send[band, rows : 2 * rows, :] = block[:, COARSE : COARSE + EDGE].astype(jnp.bfloat16)
        pairs = block[:, COARSE + EDGE :]
        if packed:
            pairs = jnp.where(lane < PAIRS, pairs[:half], pairs[half:])
        send[band, 2 * rows :, :] = pairs.astype(jnp.bfloat16)

    pl.semaphore_wait(barrier, nz * nf * 2 - 1)

    mine = my_c * nf + my_f

    def copy(first, dz, where, z, f, c, source_z, source):
        return pltpu.make_async_remote_copy(
            src_ref=send.at[f * 2 + c, pl.ds(first, last - first), :],
            dst_ref=out_ref.at[source_z, source, pl.ds(first, last - first), :],
            send_sem=send_sem.at[dz, where],
            recv_sem=recv_sem.at[source_z, source],
            device_id=(group, z, f, c),
            device_id_type=MESH,
        )

    def start(near, dz, where, z, f, c):
        if near:
            copy(0, dz, where, z, f, c, my_z, mine).start()
        else:
            @pl.when(my_c == 1)
            def _():
                copy(0, dz, where, z, f, c, my_z, mine).start()

            @pl.when(my_c == 0)
            def _():
                copy(rows, dz, where, z, f, c, my_z, mine).start()

    each_peer(start)
    own = pltpu.make_async_copy(send.at[my_f * 2 + my_c], out_ref.at[my_z, mine], own_sem)
    own.start()

    def finish(near, dz, where, z, f, c):
        if near:
            copy(0, dz, where, z, f, c, my_z, mine).wait_send()
            copy(0, dz, where, z, f, c, z, c * nf + f).wait_recv()
        else:
            for core, first in ((1, 0), (0, rows)):
                @pl.when(my_c == core)
                def _():
                    copy(first, dz, where, z, f, c, my_z, mine).wait_send()

                @pl.when(c == core)
                def _():
                    copy(first, dz, where, z, f, c, z, c * nf + f).wait_recv()

    own.wait()
    each_peer(finish)


def dot_nt(left, right):
    return lax.dot_general(left, right, (((1,), (1,)), ((), ())), preferred_element_type=jnp.float32)


def cross_kernel(
    nz, nf, rows, packed, scale,
    slots_ref, near_ref, code_ref, pair_ref, got_ref, table_ref, out_ref,
    where_ref, outer, rims, pairs, stage, sems,
):
    lanes = 2 * nf * rows
    half = rows // 2
    per_band = SEGLEN // 2 // (2 * nf)
    me = lax.axis_index("tiles")

    def place(slot):
        where_ref[slots_ref[slot]] = slot

    repeat(nz, place)

    def spread(slot):
        flat = got_ref[slot, :, rows : 2 * rows, :].reshape(lanes, EDGE)
        coded = dot_nt(table_ref[0 : 2 * EDGE, :], flat)
        outer[pl.ds(slot * 8, 8)] = coded.reshape(8, SIDE, lanes).astype(jnp.bfloat16)

    repeat(nz, spread)

    def entry(slot, edge):
        return where_ref[near_ref[slot, edge]] * 8 + code_ref[slot, edge]

    lane = lax.broadcasted_iota(jnp.int32, (1, EDGE), 1)

    def unpack(block):
        low = jnp.where(lane < PAIRS, block, jnp.zeros_like(block))
        if packed:
            return jnp.concatenate([low, jnp.where(lane < PAIRS, jnp.zeros_like(block), block)], axis=0)
        return low

    def sweep(slot):
        for edge in range(4):
            rims[slot, edge * SIDE : (edge + 1) * SIDE, :] = outer[entry(slot, edge)]
        own = jnp.concatenate([unpack(got_ref[slot, s, 2 * rows :, :]) for s in range(2 * nf)], axis=0)
        total = dot_nt(table_ref[256:384, :], own)
        total = total + jnp.dot(table_ref[384:512, :], rims[slot], preferred_element_type=jnp.float32)
        pairs[pl.ds(slot * 8, 8)] = total.reshape(8, SIDE // 2, lanes).astype(jnp.bfloat16)

    repeat(nz, sweep)

    def spectrum(slot):
        flat = got_ref[slot, :, 0:rows, :].reshape(lanes, COARSE)
        beyond = jnp.concatenate([pairs[entry(slot, edge)] for edge in range(4)], axis=0)
        total = dot_nt(table_ref[768:896, :], flat)
        total = total + jnp.dot(table_ref[512:640, :], rims[slot], preferred_element_type=jnp.float32)
        total = total + jnp.dot(table_ref[640:768, 0:PAIRS], beyond, preferred_element_type=jnp.float32)
        return total

    at = lax.broadcasted_iota(jnp.int32, (COARSE, lanes), 1)
    velocity = at >= lanes // 2
    height = spectrum(me).astype(jnp.bfloat16).astype(jnp.float32)
    height = jnp.where(velocity, pltpu.roll(height, lanes // 2, 1), 0.0)
    real_lane = at % rows < half
    turned = jnp.where(real_lane, pltpu.roll(height, lanes - half, 1), -pltpu.roll(height, half, 1))
    partner = []
    for k in range(2):
        total = spectrum(where_ref[pair_ref[0, k]])
        partner.append(jnp.where(velocity, total, 0.0).astype(jnp.bfloat16))
    partner = jnp.concatenate(partner, axis=0)
    both = jnp.concatenate([height, turned], axis=0).astype(jnp.bfloat16)
    at_both = lax.broadcasted_iota(jnp.int32, (2 * COARSE, lanes), 1) % per_band
    for f in range(per_band):
        chosen = jnp.where(at_both == f, both, jnp.zeros_like(both))
        cross = dot_nt(chosen, partner) * scale
        for k in range(2):
            for o in range(2):
                stage[f, k, o] = cross[o * COARSE : (o + 1) * COARSE, k * COARSE : (k + 1) * COARSE]
        pltpu.make_async_copy(stage.at[f], out_ref.at[0, :, :, f], sems.at[f]).start()
    for f in range(per_band):
        pltpu.make_async_copy(stage.at[f], out_ref.at[0, :, :, f], sems.at[f]).wait()


def shards(nz, nf, fields, slot_tile_ids, neighbour_tile_ids, neighbour_rotation_code, paired_tile_ids):
    samples = fields.shape[2]
    segments = samples // SEGLEN
    bands = 2 * nf
    per_band = SEGLEN // 2 // bands
    rows = 2 * segments * per_band
    lanes = bands * rows
    packed = rows % 32 == 0
    height = 2 * rows + (rows // 2 if packed else rows)
    sender, receiver = spatial_tables()
    times = time_table(segments, bands)
    scale = float(1.0 / (segments * nf * np.sum(hann() ** 2)))
    vmem = pl.BlockSpec(memory_space=pltpu.VMEM)
    smem = pl.BlockSpec(memory_space=pltpu.SMEM)
    anywhere = pl.BlockSpec(memory_space=pl.ANY)
    got = pl.pallas_call(
        functools.partial(exchange_kernel, nz, nf, rows, packed),
        out_shape=jax.ShapeDtypeStruct((nz, bands, height, EDGE), jnp.bfloat16),
        in_specs=[vmem, vmem, vmem],
        out_specs=anywhere,
        scratch_shapes=[
            pltpu.VMEM((bands, height, EDGE), jnp.bfloat16),
            pltpu.SemaphoreType.DMA((nz, bands)),
            pltpu.SemaphoreType.DMA((nz, bands)),
            pltpu.SemaphoreType.DMA,
        ],
        compiler_params=pltpu.CompilerParams(collective_id=0, has_side_effects=True),
        name="exchange",
    )(fields.reshape(samples, CELLS), jnp.asarray(sender), jnp.asarray(times))
    return pl.pallas_call(
        functools.partial(cross_kernel, nz, nf, rows, packed, scale),
        out_shape=jax.ShapeDtypeStruct((1, 2, 2, per_band, COARSE, COARSE), jnp.float32),
        in_specs=[smem, smem, smem, smem, vmem, vmem],
        out_specs=anywhere,
        scratch_shapes=[
            pltpu.SMEM((nz,), jnp.int32),
            pltpu.VMEM((nz * 8, SIDE, lanes), jnp.bfloat16),
            pltpu.VMEM((nz, EDGE, lanes), jnp.bfloat16),
            pltpu.VMEM((nz * 8, SIDE // 2, lanes), jnp.bfloat16),
            pltpu.VMEM((per_band, 2, 2, COARSE, COARSE), jnp.float32),
            pltpu.SemaphoreType.DMA((per_band,)),
        ],
        name="cross",
    )(slot_tile_ids, neighbour_tile_ids, neighbour_rotation_code, paired_tile_ids, got, jnp.asarray(receiver))


def solution(mesh):
    placed = (P("field", "tiles", ("groups", "freq"), None), P(), P(), P(), P("tiles", None))
    return jax.shard_map(
        functools.partial(shards, mesh.shape["tiles"], mesh.shape["freq"]),
        mesh=mesh,
        in_specs=placed,
        out_specs=P(("groups", "tiles"), None, None, ("freq", "field"), None, None),
        check_vma=False,
    )
```

time: 70 us -> 17.2 us (0.25)
  blocking collectives: 45.8 us -> 0 us
  Pallas kernels: 0 us -> 17 us
  local copies, waits for them, and re-layouts: 9.18 us -> 0 us
  other arithmetic: 7.23 us -> 0 us
  starting transfers between devices: 3.26 us -> 0 us
  waiting for transfers between devices: 2.42 us -> 0 us
  between operations: 1.03 us -> 0.01 us
  matrix products: 0.77 us -> 0 us
    all_gather x3 -> x0, blocking collectives: 42 us -> none  [the longest x1 15.1 us: shards(): lax.all_gather(tile_edges(field, SIDE), 'tiles', axis=0, tiled=True)]
    pallas_call x0 -> x2, Pallas kernels: none -> 17 us  [the longest x1 13.6 us: shards(): pl.pallas_call(functools.partial(exchange_kernel, nz, nf, rows, packed),...]
    all_to_all x1 -> x0, blocking collectives: 3.75 us -> none  [shards(): lax.all_to_all(lax.all_to_all(spectra[None], 'freq', split_axis=4, concat...]
    all_to_all x1 -> x0, starting transfers between devices: 3.26 us -> none  [shards(): lax.all_to_all(spectra[None], 'freq', split_axis=4, concat_axis=2, tiled=...]
    reduce_sum x4 -> x0, other arithmetic: 2.87 us -> none  [the longest x1 1.29 us: coarse_sums(): jnp.sum(blocks, axis=(-3, -1))]
    convert_element_type x9 -> x0, other arithmetic: 2.62 us -> none  [the longest x2 2.21 us: smooth_step(): values = field.astype(jnp.float32)]
    slice x12 -> x0, local copies, waits for them, and re-layouts: 2.45 us -> none  [the longest x1 1.02 us: smooth_step(): values[..., :cell_count - tile_side]]
    all_to_all x1 -> x0, waiting for transfers between devices: 2.42 us -> none  [shards(): lax.all_to_all(spectra[None], 'freq', split_axis=4, concat_axis=2, tiled=...]
  transfers between devices with their start and end apart: 1 -> 0, of which waited for: 1 -> 0; matrix products, arithmetic and copies ran while one was open for 1% -> 0% of each run, Pallas kernels for 0% -> 0%
where the time goes in v1:
time: 17.2 us; the launch traced here: 17 us
  Pallas kernels  17 us (99%)
    pallas_call x1, Pallas kernels, shards(): pl.pallas_call(functools.partial(exchange_kernel, nz, nf, rows, packed),...  13.6 us
    pallas_call x1, Pallas kernels, shards(): pl.pallas_call(functools.partial(cross_kernel, nz, nf, rows, packed, scal...  3.4 us

profile of v1, /device:TPU:0, one launch (start us, length us, event | category | flops | bytes accessed | tf_op | source)
XLA Modules:
  0.0 17.0 jit_solution(15274468216708445016)
XLA Ops:
  0.0 13.6 %exchange.1.got_ref = bf16[4,4,80,128]{3,2,1,0:T(8,128)(2,1)} custom-call(bf16[128,1024]{1,0:T(8,128)(2,1)} %bitcast.1, bf16[1024,384]{1,0:T(8,128)(2,1)} %constant.6.clone.spatial_ref, f32[128,128]{1,0:T(8,128)} %constant.7.clone.time_ref), custom_call_target="tpu_custom_call" | custom-call | tf_op jit(solution)/shard_map/exchange/pallas_call | solution.py:286
  13.6 3.4 %cross.1 = f32[1,2,2,8,128,128]{5,4,3,2,1,0:T(8,128)} custom-call(s32[4]{0:T(128)} %slots_ref.1, s32[4,4]{1,0:T(4,128)} %near_ref.1, s32[4,4]{1,0:T(4,128)} %code_ref.1, s32[1,2]{1,0:T(1,128)} %pair_ref.1, bf16[4,4,80,128]{3,2,1,0:T(8,128)(2,1)} %exchange.1.got_ref, bf16[896,128]{1,0:T(8,128)(2,1)} %constant.8.clone.table_ref), custom_call_target="tpu_custom_call" | custom-call | tf_op jit(solution)/shard_map/cross/pallas_call | solution.py:300

commit v2 on v1

--- a/solution.py
+++ b/solution.py
@@ -14,6 +14,7 @@
 EDGE = 4 * SIDE
 PAIRS = EDGE // 2
 COARSE = CELLS // 8
+CHUNKS = 2
 MESH = pl.DeviceIdType.MESH
 
 
@@ -83,7 +84,10 @@
             for segment in range(segments):
                 table[band, 0, segment, inner, segment] = window * np.cos(angles)
                 table[band, 1, segment, inner, segment] = -window * np.sin(angles)
-    return table.reshape(bands * 2 * segments * per_band, segments * SEGLEN).astype(np.float32)
+    table = table.reshape(bands * 2 * segments * per_band, segments * SEGLEN).astype(np.float32)
+    upper = table.astype(jnp.bfloat16)
+    lower = (table - upper.astype(np.float32)).astype(jnp.bfloat16)
+    return np.concatenate([upper, lower, upper], axis=1)
 
 
 def repeat(count, body):
@@ -94,7 +98,9 @@
         lax.fori_loop(0, count, lambda step, carry: (body(step), carry)[1], 0)
 
 
-def exchange_kernel(nz, nf, rows, packed, field_ref, spatial_ref, time_ref, out_ref, send, send_sem, recv_sem, own_sem):
+def exchange_kernel(nz, nf, rows, packed, field_hbm, spatial_hbm, time_hbm, *refs):
+    kept, (out_ref, *copies) = refs[:5], refs[5:11]
+    field_ref, spatial_ref, time_ref, send, send_sem, recv_sem, load_sem, own_sem, keep_sem = refs[11:]
     group = lax.axis_index("groups")
     my_z = lax.axis_index("tiles")
     my_f = lax.axis_index("freq")
@@ -126,9 +132,32 @@
 
     each_peer(greet)
 
-    mapped = jnp.dot(field_ref[...], spatial_ref[...], preferred_element_type=jnp.float32)
+    loads = []
+    for chunk in range(CHUNKS):
+        cells = pl.ds(chunk * CELLS // CHUNKS, CELLS // CHUNKS)
+        loads.append((
+            pltpu.make_async_copy(field_hbm.at[:, cells], field_ref.at[:, cells], load_sem.at[2 * chunk]),
+            pltpu.make_async_copy(spatial_hbm.at[cells, :], spatial_ref.at[cells, :], load_sem.at[2 * chunk + 1]),
+        ))
+    loads.append((pltpu.make_async_copy(time_hbm, time_ref, load_sem.at[2 * CHUNKS]),))
+    for load in loads:
+        for part in load:
+            part.start()
+    keeps = [pltpu.make_async_copy(a, b, keep_sem.at[i]) for i, (a, b) in enumerate(zip(kept, copies))]
+    for keep in keeps:
+        keep.start()
+    mapped = None
+    for chunk in range(CHUNKS):
+        for part in loads[chunk]:
+            part.wait()
+        cells = pl.ds(chunk * CELLS // CHUNKS, CELLS // CHUNKS)
+        term = jnp.dot(field_ref[:, cells], spatial_ref[cells, :], preferred_element_type=jnp.float32)
+        mapped = term if mapped is None else mapped + term
+    loads[CHUNKS][0].wait()
+    upper = mapped.astype(jnp.bfloat16)
+    lower = (mapped - upper.astype(jnp.float32)).astype(jnp.bfloat16)
     spectra = jnp.dot(
-        time_ref[...], mapped, precision=lax.Precision.HIGHEST, preferred_element_type=jnp.float32
+        time_ref[...], jnp.concatenate([upper, upper, lower], axis=0), preferred_element_type=jnp.float32
     )
     half = rows // 2
     lane = lax.broadcasted_iota(jnp.int32, (half, EDGE), 1)
@@ -186,6 +215,8 @@
                     copy(first, dz, where, z, f, c, z, c * nf + f).wait_recv()
 
     own.wait()
+    for keep in keeps:
+        keep.wait()
     each_peer(finish)
 
 
@@ -282,21 +313,33 @@
     scale = float(1.0 / (segments * nf * np.sum(hann() ** 2)))
     vmem = pl.BlockSpec(memory_space=pltpu.VMEM)
     smem = pl.BlockSpec(memory_space=pltpu.SMEM)
+    hbm = pl.BlockSpec(memory_space=pltpu.HBM)
     anywhere = pl.BlockSpec(memory_space=pl.ANY)
-    got = pl.pallas_call(
+    ids = (slot_tile_ids, neighbour_tile_ids, neighbour_rotation_code, paired_tile_ids)
+    kept = ids + (jnp.asarray(receiver),)
+    got, *kept = pl.pallas_call(
         functools.partial(exchange_kernel, nz, nf, rows, packed),
-        out_shape=jax.ShapeDtypeStruct((nz, bands, height, EDGE), jnp.bfloat16),
-        in_specs=[vmem, vmem, vmem],
-        out_specs=anywhere,
+        out_shape=[jax.ShapeDtypeStruct((nz, bands, height, EDGE), jnp.bfloat16)]
+        + [jax.ShapeDtypeStruct(a.shape, a.dtype) for a in kept],
+        in_specs=[hbm] * 8,
+        out_specs=[anywhere] * 6,
         scratch_shapes=[
+            pltpu.VMEM((samples, CELLS), jnp.bfloat16),
+            pltpu.VMEM(sender.shape, jnp.bfloat16),
+            pltpu.VMEM(times.shape, jnp.bfloat16),
             pltpu.VMEM((bands, height, EDGE), jnp.bfloat16),
             pltpu.SemaphoreType.DMA((nz, bands)),
             pltpu.SemaphoreType.DMA((nz, bands)),
+            pltpu.SemaphoreType.DMA((2 * CHUNKS + 1,)),
             pltpu.SemaphoreType.DMA,
+            pltpu.SemaphoreType.DMA((5,)),
         ],
-        compiler_params=pltpu.CompilerParams(collective_id=0, has_side_effects=True),
+        compiler_params=pltpu.CompilerParams(
+            collective_id=0, has_side_effects=True, vmem_limit_bytes=4 << 20
+        ),
         name="exchange",
-    )(fields.reshape(samples, CELLS), jnp.asarray(sender), jnp.asarray(times))
+    )(*[pltpu.with_memory_space_constraint(a, pltpu.HBM) for a in
+         (fields.reshape(samples, CELLS), jnp.asarray(sender), jnp.asarray(times), *kept)])
     return pl.pallas_call(
         functools.partial(cross_kernel, nz, nf, rows, packed, scale),
         out_shape=jax.ShapeDtypeStruct((1, 2, 2, per_band, COARSE, COARSE), jnp.float32),
@@ -310,8 +353,9 @@
             pltpu.VMEM((per_band, 2, 2, COARSE, COARSE), jnp.float32),
             pltpu.SemaphoreType.DMA((per_band,)),
         ],
+        compiler_params=pltpu.CompilerParams(vmem_limit_bytes=max(8, nz) << 20),
         name="cross",
-    )(slot_tile_ids, neighbour_tile_ids, neighbour_rotation_code, paired_tile_ids, got, jnp.asarray(receiver))
+    )(*kept[:4], got, kept[4])
 
 
 def solution(mesh):

time: 17.2 us -> 15.5 us (0.901)
  Pallas kernels: 17 us -> 15.4 us
    pallas_call x1, Pallas kernels: 13.6 us -> 12.4 us  [shards(): pl.pallas_call(functools.partial(exchange_kernel, nz, nf, rows, packed),...]
    pallas_call x1, Pallas kernels: 3.4 us -> 2.97 us  [shards(): pl.pallas_call(functools.partial(cross_kernel, nz, nf, rows, packed, scal...]
where the time goes in v2:
time: 15.5 us; the launch traced here: 15.4 us
  Pallas kernels  15.4 us (99%)
    pallas_call x1, Pallas kernels, shards(): pl.pallas_call(functools.partial(exchange_kernel, nz, nf, rows, packed),...  12.4 us
    pallas_call x1, Pallas kernels, shards(): pl.pallas_call(functools.partial(cross_kernel, nz, nf, rows, packed, scal...  2.97 us

profile of v2, /device:TPU:0, one launch (start us, length us, event | category | flops | bytes accessed | tf_op | source)
XLA Modules:
  0.0 15.4 jit_solution(1479364411263127869)
XLA Ops:
  0.0 12.4 %exchange.1 = (bf16[4,4,80,128]{3,2,1,0:T(8,128)(2,1)S(1)}, s32[4]{0:T(128)S(1)}, s32[4,4]{1,0:T(4,128)S(1)}, s32[4,4]{1,0:T(4,128)S(1)}, s32[1,2]{1,0:T(1,128)S(1)}, /*index=5*/bf16[896,128]{1,0:T(8,128)(2,1)S(1)}) custom-call(bf16[128,1024]{1,0:T(8,128)(2,1)} %bitcast.1, bf16[1024,384]{1,0:T(8,128)(2,1)} %constant.7.clone.spatial_hbm, ...), custom_call_target="tpu_custom_call" | custom-call | tf_op jit(solution)/shard_map/exchange/pallas_call | solution.py:320
  12.4 3.0 %cross.1 = f32[1,2,2,8,128,128]{5,4,3,2,1,0:T(8,128)} custom-call(s32[4]{0:T(128)S(1)} %get-tuple-element.11.slots_ref, s32[4,4]{1,0:T(4,128)S(1)} %get-tuple-element.12.near_ref, s32[4,4]{1,0:T(4,128)S(1)} %get-tuple-element.13.code_ref, s32[1,2]{1,0:T(1,128)S(1)} %get-tuple-element.14.pair_ref, bf16[4,4,80,128]{3,2,1,0:T(8,128)(2,1)S(1)} %get-tuple-element.15.got_ref, ...), custom_call_target="tpu_custom_call" | custom-call | tf_op jit(solution)/shard_map/cross/pallas_call | solution.py:343

commit v3 on v2

--- a/solution.py
+++ b/solution.py
@@ -122,15 +122,14 @@
             if where:
                 visit(True, dz, where, z, f, c)
 
+        repeat(nz - 1, lambda step: peers(step + 1, functools.partial(visit, False)))
         peers(0, same)
-        repeat(nz - 1, lambda step: peers(step + 1, functools.partial(visit, False)))
 
     barrier = pltpu.get_barrier_semaphore()
 
     def greet(near, dz, where, z, f, c):
         pl.semaphore_signal(barrier, inc=1, device_id=(group, z, f, c), device_id_type=MESH)
 
-    each_peer(greet)
 
     loads = []
     for chunk in range(CHUNKS):
@@ -143,9 +142,8 @@
     for load in loads:
         for part in load:
             part.start()
+    each_peer(greet)
     keeps = [pltpu.make_async_copy(a, b, keep_sem.at[i]) for i, (a, b) in enumerate(zip(kept, copies))]
-    for keep in keeps:
-        keep.start()
     mapped = None
     for chunk in range(CHUNKS):
         for part in loads[chunk]:
@@ -154,6 +152,8 @@
         term = jnp.dot(field_ref[:, cells], spatial_ref[cells, :], preferred_element_type=jnp.float32)
         mapped = term if mapped is None else mapped + term
     loads[CHUNKS][0].wait()
+    for keep in keeps:
+        keep.start()
     upper = mapped.astype(jnp.bfloat16)
     lower = (mapped - upper.astype(jnp.float32)).astype(jnp.bfloat16)
     spectra = jnp.dot(

time: 15.5 us -> 15.5 us (level)
  no operation moved by 1% of the time
where the time goes in v3:
time: 15.5 us; the launch traced here: 15.3 us
  Pallas kernels  15.3 us (99%)
    pallas_call x1, Pallas kernels, shards(): pl.pallas_call(functools.partial(exchange_kernel, nz, nf, rows, packed),...  12.3 us
    pallas_call x1, Pallas kernels, shards(): pl.pallas_call(functools.partial(cross_kernel, nz, nf, rows, packed, scal...  2.97 us

profile of v3, /device:TPU:0, one launch (start us, length us, event | category | flops | bytes accessed | tf_op | source)
XLA Modules:
  0.0 15.3 jit_solution(13445987660102160084)
XLA Ops:
  0.0 12.3 %exchange.1 = (bf16[4,4,80,128]{3,2,1,0:T(8,128)(2,1)S(1)}, s32[4]{0:T(128)S(1)}, s32[4,4]{1,0:T(4,128)S(1)}, s32[4,4]{1,0:T(4,128)S(1)}, s32[1,2]{1,0:T(1,128)S(1)}, /*index=5*/bf16[896,128]{1,0:T(8,128)(2,1)S(1)}) custom-call(bf16[128,1024]{1,0:T(8,128)(2,1)} %bitcast.1, bf16[1024,384]{1,0:T(8,128)(2,1)} %constant.7.clone.spatial_hbm, ...), custom_call_target="tpu_custom_call" | custom-call | tf_op jit(solution)/shard_map/exchange/pallas_call | solution.py:320
  12.3 3.0 %cross.1 = f32[1,2,2,8,128,128]{5,4,3,2,1,0:T(8,128)} custom-call(s32[4]{0:T(128)S(1)} %get-tuple-element.11.slots_ref, s32[4,4]{1,0:T(4,128)S(1)} %get-tuple-element.12.near_ref, s32[4,4]{1,0:T(4,128)S(1)} %get-tuple-element.13.code_ref, s32[1,2]{1,0:T(1,128)S(1)} %get-tuple-element.14.pair_ref, bf16[4,4,80,128]{3,2,1,0:T(8,128)(2,1)S(1)} %get-tuple-element.15.got_ref, ...), custom_call_target="tpu_custom_call" | custom-call | tf_op jit(solution)/shard_map/cross/pallas_call | solution.py:343

commit v4 on v3

--- a/solution.py
+++ b/solution.py
@@ -281,22 +281,23 @@
     height = jnp.where(velocity, pltpu.roll(height, lanes // 2, 1), 0.0)
     real_lane = at % rows < half
     turned = jnp.where(real_lane, pltpu.roll(height, lanes - half, 1), -pltpu.roll(height, half, 1))
-    partner = []
+    both = jnp.concatenate([height, turned], axis=0).astype(jnp.bfloat16)
+    at_both = lax.broadcasted_iota(jnp.int32, (2 * COARSE, lanes), 1) % per_band
     for k in range(2):
         total = spectrum(where_ref[pair_ref[0, k]])
-        partner.append(jnp.where(velocity, total, 0.0).astype(jnp.bfloat16))
-    partner = jnp.concatenate(partner, axis=0)
-    both = jnp.concatenate([height, turned], axis=0).astype(jnp.bfloat16)
-    at_both = lax.broadcasted_iota(jnp.int32, (2 * COARSE, lanes), 1) % per_band
-    for f in range(per_band):
-        chosen = jnp.where(at_both == f, both, jnp.zeros_like(both))
-        cross = dot_nt(chosen, partner) * scale
-        for k in range(2):
+        partner = jnp.where(velocity, total, 0.0).astype(jnp.bfloat16)
+        for f in range(per_band):
+            chosen = jnp.where(at_both == f, both, jnp.zeros_like(both))
+            cross = dot_nt(chosen, partner) * scale
             for o in range(2):
-                stage[f, k, o] = cross[o * COARSE : (o + 1) * COARSE, k * COARSE : (k + 1) * COARSE]
-        pltpu.make_async_copy(stage.at[f], out_ref.at[0, :, :, f], sems.at[f]).start()
-    for f in range(per_band):
-        pltpu.make_async_copy(stage.at[f], out_ref.at[0, :, :, f], sems.at[f]).wait()
+                stage[k, o, f] = cross[o * COARSE : (o + 1) * COARSE]
+            if f % 4 == 3:
+                part = (k, slice(None), pl.ds(f - 3, 4))
+                pltpu.make_async_copy(stage.at[part], out_ref.at[(0, *part)], sems.at[k, f // 4]).start()
+    for k in range(2):
+        for f in range(0, per_band, 4):
+            part = (k, slice(None), pl.ds(f, 4))
+            pltpu.make_async_copy(stage.at[part], out_ref.at[(0, *part)], sems.at[k, f // 4]).wait()
 
 
 def shards(nz, nf, fields, slot_tile_ids, neighbour_tile_ids, neighbour_rotation_code, paired_tile_ids):
@@ -350,8 +351,8 @@
             pltpu.VMEM((nz * 8, SIDE, lanes), jnp.bfloat16),
             pltpu.VMEM((nz, EDGE, lanes), jnp.bfloat16),
             pltpu.VMEM((nz * 8, SIDE // 2, lanes), jnp.bfloat16),
-            pltpu.VMEM((per_band, 2, 2, COARSE, COARSE), jnp.float32),
-            pltpu.SemaphoreType.DMA((per_band,)),
+            pltpu.VMEM((2, 2, per_band, COARSE, COARSE), jnp.float32),
+            pltpu.SemaphoreType.DMA((2, per_band // 4)),
         ],
         compiler_params=pltpu.CompilerParams(vmem_limit_bytes=max(8, nz) << 20),
         name="cross",

time: 15.5 us -> 15.5 us (level)
  no operation moved by 1% of the time
where the time goes in v4:
time: 15.5 us; the launch traced here: 15.3 us
  Pallas kernels  15.3 us (99%)
    pallas_call x1, Pallas kernels, shards(): pl.pallas_call(functools.partial(exchange_kernel, nz, nf, rows, packed),...  12.3 us
    pallas_call x1, Pallas kernels, shards(): pl.pallas_call(functools.partial(cross_kernel, nz, nf, rows, packed, scal...  2.98 us

profile of v4, /device:TPU:0, one launch (start us, length us, event | category | flops | bytes accessed | tf_op | source)
XLA Modules:
  0.0 15.3 jit_solution(5794519594332341654)
XLA Ops:
  0.0 12.3 %exchange.1 = (bf16[4,4,80,128]{3,2,1,0:T(8,128)(2,1)S(1)}, s32[4]{0:T(128)S(1)}, s32[4,4]{1,0:T(4,128)S(1)}, s32[4,4]{1,0:T(4,128)S(1)}, s32[1,2]{1,0:T(1,128)S(1)}, /*index=5*/bf16[896,128]{1,0:T(8,128)(2,1)S(1)}) custom-call(bf16[128,1024]{1,0:T(8,128)(2,1)} %bitcast.1, bf16[1024,384]{1,0:T(8,128)(2,1)} %constant.7.clone.spatial_hbm, ...), custom_call_target="tpu_custom_call" | custom-call | tf_op jit(solution)/shard_map/exchange/pallas_call | solution.py:321
  12.3 3.0 %cross.1 = f32[1,2,2,8,128,128]{5,4,3,2,1,0:T(8,128)} custom-call(s32[4]{0:T(128)S(1)} %get-tuple-element.11.slots_ref, s32[4,4]{1,0:T(4,128)S(1)} %get-tuple-element.12.near_ref, s32[4,4]{1,0:T(4,128)S(1)} %get-tuple-element.13.code_ref, s32[1,2]{1,0:T(1,128)S(1)} %get-tuple-element.14.pair_ref, bf16[4,4,80,128]{3,2,1,0:T(8,128)(2,1)S(1)} %get-tuple-element.15.got_ref, ...), custom_call_target="tpu_custom_call" | custom-call | tf_op jit(solution)/shard_map/cross/pallas_call | solution.py:344
